TPU v7x, 512 devices: a whole 4x4x16 slice. The times are simulated.
512 devices in a mesh: mx: 16 (over y, z_hi), my: 16 (over x, z_lo), dz: 2 (over core).
Axes of the slice: x: 4, y: 4, z: 16 (z_hi: 4, z_lo: 4; z = z_hi * 4 + z_lo), core: 2. Of those that a mesh axis runs over, the one named last changes fastest.
Arguments:
- electric: float32 [3, 16, 256, 2048], P(None, 'dz', 'mx', 'my'), may hold values from -6 to 6
- magnetic: float32 [3, 16, 256, 2048], P(None, 'dz', 'mx', 'my'), may hold values from -6 to 6
- poles: float32 [3, 3, 16, 256, 2048], P(None, None, 'dz', 'mx', 'my'), may hold values from -4 to 4
- material: int32 [16, 256, 2048], P('dz', 'mx', 'my'), may hold values from 0 to 3
- exit_layer: int32 [1], replicated, may hold values from 0 to 15
Outputs:
- electric_next: float32 [3, 16, 256, 2048], P(None, 'dz', 'mx', 'my')
- magnetic_next: float32 [3, 16, 256, 2048], P(None, 'dz', 'mx', 'my')
- poles_next: float32 [3, 3, 16, 256, 2048], P(None, None, 'dz', 'mx', 'my')
- far_field: float32 [4, 2, 2, 128, 128], P('dz', None, None, 'mx', 'my')
All inputs are finite; a program needn't handle non-finite values.
Results may differ from a plain program's by a relative error of at most 0.00016.
Values sent between devices are 32-bit elements; how exact they have to be, the bound alone decides.
A program may use at most 64 MiB of HBM per device.

v0:
```python
import math
import jax
import jax.numpy as jnp
import numpy as np
from jax import lax
from jax.sharding import PartitionSpec as P

STEPS = 4
W = 4
U = 128
V = 128
time_step = 0.5
eps_inf = np.array([1.0, 4.0, 2.1, 1.5])
drude_plasma = np.array([0.0, 0.0, 0.0, 2.0])
drude_damping = np.array([0.0, 0.0, 0.0, 0.1])
lorentz_square = np.array([0.3, 0.8, 1.0, 0.5])
lorentz_strength = np.array([0.0, 1.5, 0.1, 0.8])
lorentz_damping = np.array([0.0, 0.05, 0.02, 0.2])
drude_keep = (1.0 - drude_damping * time_step / 2) / (1.0 + drude_damping * time_step / 2)
drude_drive = drude_plasma * time_step / (1.0 + drude_damping * time_step / 2)
lorentz_keep = (1.0 - lorentz_damping * time_step / 2) / (1.0 + lorentz_damping * time_step / 2)
lorentz_push = time_step / (1.0 + lorentz_damping * time_step / 2)
coef_table = np.stack(
    [
        drude_keep,
        drude_drive,
        lorentz_keep,
        lorentz_push * lorentz_square * lorentz_strength,
        lorentz_push * lorentz_square,
        time_step / eps_inf,
    ]
).astype(np.float32)


def from_behind(x, axis, by):
    devices = lax.axis_size(axis)
    pairs = [(i, i + by) for i in range(devices) if 0 <= i + by < devices]
    return lax.ppermute(x, axis, pairs)


def coefficients(material):
    result = []
    for row in range(6):
        value = jnp.zeros(material.shape, jnp.float32)
        for which in range(4):
            value = value + jnp.where(
                material == which, jnp.float32(coef_table[row, which]), jnp.float32(0.0)
            )
        result.append(value)
    return result


def first_layer(field, axis):
    return lax.slice_in_dim(field, 0, 1, axis=axis)


def last_layer(field, axis):
    return lax.slice_in_dim(field, field.shape[axis] - 1, field.shape[axis], axis=axis)


def rim_forward(field, rim, axis):
    inner = lax.slice_in_dim(field, 1, field.shape[axis], axis=axis)
    return jnp.concatenate([inner, rim], axis) - field


def rim_backward(field, rim, axis):
    inner = lax.slice_in_dim(field, 0, field.shape[axis] - 1, axis=axis)
    return field - jnp.concatenate([rim, inner], axis)


def curl_electric(electric):
    part_x, part_y, part_z = (electric[0], electric[1], electric[2])
    xrim_y, xrim_z = from_behind((first_layer(part_y, 1), first_layer(part_z, 1)), "mx", -1)
    yrim_x, yrim_z = from_behind((first_layer(part_x, 2), first_layer(part_z, 2)), "my", -1)
    zrim_x, zrim_y = from_behind((first_layer(part_x, 0), first_layer(part_y, 0)), "dz", -1)
    return jnp.stack(
        [
            rim_forward(part_z, yrim_z, 2) - rim_forward(part_y, zrim_y, 0),
            rim_forward(part_x, zrim_x, 0) - rim_forward(part_z, xrim_z, 1),
            rim_forward(part_y, xrim_y, 1) - rim_forward(part_x, yrim_x, 2),
        ]
    )


def curl_magnetic(magnetic):
    part_x, part_y, part_z = (magnetic[0], magnetic[1], magnetic[2])
    xrim_y, xrim_z = from_behind((last_layer(part_y, 1), last_layer(part_z, 1)), "mx", 1)
    yrim_x, yrim_z = from_behind((last_layer(part_x, 2), last_layer(part_z, 2)), "my", 1)
    zrim_x, zrim_y = from_behind((last_layer(part_x, 0), last_layer(part_y, 0)), "dz", 1)
    return jnp.stack(
        [
            rim_backward(part_z, yrim_z, 2) - rim_backward(part_y, zrim_y, 0),
            rim_backward(part_x, zrim_x, 0) - rim_backward(part_z, xrim_z, 1),
            rim_backward(part_y, xrim_y, 1) - rim_backward(part_x, yrim_x, 2),
        ]
    )


def phase_tables(waves, total_steps):
    period = (8 + 2 * waves).astype(jnp.float32)
    moments = jnp.arange(1, total_steps + 1).astype(jnp.float32)
    angle = 2 * math.pi * moments[None, :] / period[:, None]
    return (jnp.cos(angle), jnp.sin(angle))


def transform_table(waves, outputs, positions, center, scale):
    rows = jnp.arange(outputs) - outputs // 2
    product = rows[:, None] * (positions - center)[None, :]
    period = outputs * (5 + waves)
    folded = jnp.mod(product[None, :, :], period[:, None, None])
    angle = 2 * math.pi * folded.astype(jnp.float32) / period.astype(jnp.float32)[:, None, None]
    return (scale * jnp.cos(angle), -scale * jnp.sin(angle))


def product_of(form, left, right):
    return jnp.einsum(form, left, right, precision=lax.Precision.HIGHEST)


def along_rows(kern_re, kern_im, data_re, data_im):
    form = "wux,wpxy->wpuy"
    real = product_of(form, kern_re, data_re) - product_of(form, kern_im, data_im)
    imag = product_of(form, kern_re, data_im) + product_of(form, kern_im, data_re)
    return (real, imag)


def along_columns(data_re, data_im, kern_re, kern_im):
    form = "wpuy,wvy->wpuv"
    real = product_of(form, data_re, kern_re) - product_of(form, data_im, kern_im)
    imag = product_of(form, data_im, kern_re) + product_of(form, data_re, kern_im)
    return (real, imag)


def body(electric, magnetic, poles, material, exit_layer):
    depth, cells_x, cells_y = material.shape
    keep_d, drive_d, keep_l, drive_l, restore_l, scale_e = coefficients(material)
    depth_index = lax.axis_index("dz") * depth + jnp.arange(depth)
    selector = (depth_index == exit_layer[0]).astype(jnp.float32)
    polar, current, drude = (poles[0], poles[1], poles[2])
    planes = []
    for _ in range(STEPS):
        magnetic = magnetic - time_step * curl_electric(electric)
        current_new = keep_l * current + drive_l * electric - restore_l * polar
        polar = polar + time_step * current_new
        drude_new = keep_d * drude + drive_d * electric
        electric = electric + scale_e * (
            curl_magnetic(magnetic) - 0.5 * (drude + drude_new) - current_new
        )
        current, drude = (current_new, drude_new)
        planes.append(product_of("z,czxy->cxy", selector, electric[:2]))
    planes = jnp.stack(planes)
    cos_t, sin_t = phase_tables(jnp.arange(W), STEPS)
    phasor = jnp.stack(
        [product_of("wn,npxy->wpxy", cos_t, planes), -product_of("wn,npxy->wpxy", sin_t, planes)], 1
    )
    mine = lax.psum_scatter(phasor, "dz", scatter_dimension=0, tiled=True)
    local_waves = mine.shape[0]
    waves = lax.axis_index("dz") * local_waves + jnp.arange(local_waves).astype(jnp.int32)
    total_x = cells_x * lax.axis_size("mx")
    total_y = cells_y * lax.axis_size("my")
    pos_x = lax.axis_index("mx") * cells_x + jnp.arange(cells_x)
    pos_y = lax.axis_index("my") * cells_y + jnp.arange(cells_y)
    row_re, row_im = transform_table(waves, U, pos_x, total_x // 2, 1.0 / math.sqrt(total_x))
    col_re, col_im = transform_table(waves, V, pos_y, total_y // 2, 1.0 / math.sqrt(total_y))
    mid_re, mid_im = along_rows(row_re, row_im, mine[:, 0], mine[:, 1])
    rows_share = U // lax.axis_size("mx")
    cols_share = V // lax.axis_size("my")
    far_re, far_im = along_columns(mid_re, mid_im, col_re, col_im)
    total = lax.psum(jnp.stack([far_re, far_im], 1), ("mx", "my"))
    total = lax.dynamic_slice_in_dim(total, lax.axis_index("mx") * rows_share, rows_share, 3)
    far_field = lax.dynamic_slice_in_dim(total, lax.axis_index("my") * cols_share, cols_share, 4)
    poles_next = jnp.stack([polar, current, drude])
    return (electric, magnetic, poles_next, far_field)


def solution(mesh):
    return jax.shard_map(
        body,
        mesh=mesh,
        in_specs=(
            P(None, "dz", "mx", "my"),
            P(None, "dz", "mx", "my"),
            P(None, None, "dz", "mx", "my"),
            P("dz", "mx", "my"),
            P(),
        ),
        out_specs=(
            P(None, "dz", "mx", "my"),
            P(None, "dz", "mx", "my"),
            P(None, None, "dz", "mx", "my"),
            P("dz", None, None, "mx", "my"),
        ),
        check_vma=False,
    )
```

profile of v0, /device:TPU:4, one launch (start us, length us, event | category | flops | bytes accessed | tf_op | source)
XLA Modules:
  0.0 669.9 jit_solution(14490689699884551274)
XLA Ops:
  8.2 6.5 collective-permute-start
  16.0 2.0 collective-permute-start.5
  23.9 1.5 collective-permute-done.3
  25.4 4.0 collective-permute-done.4
  30.5 3.8 collective-permute-start.6
  34.3 7.8 %collective-permute-start.9 = (f32[8,1,128]{2,1,0:T(1,128)S(1)}, f32[8,1,128]{2,1,0:T(1,128)S(1)}, u32[]{:S(2)}, u32[]{:S(2)}) collective-permute-start(f32[8,1,128]{2,1,0:T(1,128)S(1)} %slice.645), channel_id=1, source_target_pairs={{0,32},{32,64},{64,96},{96,128},{128,160},{160,192},{192,224},{224... | collective-permute-start | bytes 12296 | tf_op jit(solution)/shard_map/ppermute | solution.py:38
  45.7 2.1 collective-permute-start.11
  47.8 7.8 %collective-permute-start.10 = (f32[8,1,128]{2,1,0:T(1,128)S(1)}, f32[8,1,128]{2,1,0:T(1,128)S(1)}, u32[]{:S(2)}, u32[]{:S(2)}) collective-permute-start(f32[8,1,128]{2,1,0:T(1,128)S(1)} %slice.647), channel_id=1, source_target_pairs={{0,32},{32,64},{64,96},{96,128},{128,160},{160,192},{192,224},{224... | collective-permute-start | bytes 12296 | tf_op jit(solution)/shard_map/ppermute | solution.py:38
  57.3 6.6 collective-permute-start.12
  63.9 1.3 collective-permute-start.15
  65.2 1.3 collective-permute-start.13
  66.5 1.3 collective-permute-start.14
  68.1 5.5 collective-permute-done.15
  73.7 2.1 collective-permute-start.17
  77.2 2.7 collective-permute-done.17
  79.9 5.7 collective-permute-done.16
  85.9 3.4 collective-permute-start.18
  89.3 7.8 %collective-permute-start.21 = (f32[8,1,128]{2,1,0:T(1,128)S(1)}, f32[8,1,128]{2,1,0:T(1,128)S(1)}, u32[]{:S(2)}, u32[]{:S(2)}) collective-permute-start(f32[8,1,128]{2,1,0:T(1,128)S(1)} %slice.675), channel_id=1, source_target_pairs={{0,32},{32,64},{64,96},{96,128},{128,160},{160,192},{192,224},{224... | collective-permute-start | bytes 12296 | tf_op jit(solution)/shard_map/ppermute | solution.py:38
  100.7 1.9 collective-permute-start.23
  102.7 7.3 %collective-permute-start.22 = (f32[8,1,128]{2,1,0:T(1,128)S(1)}, f32[8,1,128]{2,1,0:T(1,128)S(1)}, u32[]{:S(2)}, u32[]{:S(2)}) collective-permute-start(f32[8,1,128]{2,1,0:T(1,128)S(1)} %slice.677), channel_id=1, source_target_pairs={{0,32},{32,64},{64,96},{96,128},{128,160},{160,192},{192,224},{224... | collective-permute-start | bytes 12296 | tf_op jit(solution)/shard_map/ppermute | solution.py:38
  111.6 6.6 collective-permute-start.24
  118.2 1.3 collective-permute-start.27
  119.5 1.3 collective-permute-start.25
  120.8 1.3 collective-permute-start.26
  122.5 6.0 collective-permute-done.27
  128.6 3.0 collective-permute-start.29
  132.9 1.9 collective-permute-done.29
  134.8 6.5 collective-permute-done.28
  141.6 2.9 collective-permute-start.30
  144.5 7.8 %collective-permute-start.33 = (f32[8,1,128]{2,1,0:T(1,128)S(1)}, f32[8,1,128]{2,1,0:T(1,128)S(1)}, u32[]{:S(2)}, u32[]{:S(2)}) collective-permute-start(f32[8,1,128]{2,1,0:T(1,128)S(1)} %slice.705), channel_id=1, source_target_pairs={{0,32},{32,64},{64,96},{96,128},{128,160},{160,192},{192,224},{224... | collective-permute-start | bytes 12296 | tf_op jit(solution)/shard_map/ppermute | solution.py:38
  155.9 1.9 collective-permute-start.35
  157.9 7.8 %collective-permute-start.34 = (f32[8,1,128]{2,1,0:T(1,128)S(1)}, f32[8,1,128]{2,1,0:T(1,128)S(1)}, u32[]{:S(2)}, u32[]{:S(2)}) collective-permute-start(f32[8,1,128]{2,1,0:T(1,128)S(1)} %slice.707), channel_id=1, source_target_pairs={{0,32},{32,64},{64,96},{96,128},{128,160},{160,192},{192,224},{224... | collective-permute-start | bytes 12296 | tf_op jit(solution)/shard_map/ppermute | solution.py:38
  167.4 6.6 collective-permute-start.36
  178.3 5.5 collective-permute-done.39
  183.9 3.0 collective-permute-start.41
  188.2 1.9 collective-permute-done.41
  190.1 6.2 collective-permute-done.40
  196.6 2.9 collective-permute-start.42
  199.5 7.8 %collective-permute-start.45 = (f32[8,1,128]{2,1,0:T(1,128)S(1)}, f32[8,1,128]{2,1,0:T(1,128)S(1)}, u32[]{:S(2)}, u32[]{:S(2)}) collective-permute-start(f32[8,1,128]{2,1,0:T(1,128)S(1)} %slice.735), channel_id=1, source_target_pairs={{0,32},{32,64},{64,96},{96,128},{128,160},{160,192},{192,224},{224... | collective-permute-start | bytes 12296 | tf_op jit(solution)/shard_map/ppermute | solution.py:38
  211.0 1.9 collective-permute-start.47
  212.9 7.8 %collective-permute-start.46 = (f32[8,1,128]{2,1,0:T(1,128)S(1)}, f32[8,1,128]{2,1,0:T(1,128)S(1)}, u32[]{:S(2)}, u32[]{:S(2)}) collective-permute-start(f32[8,1,128]{2,1,0:T(1,128)S(1)} %slice.737), channel_id=1, source_target_pairs={{0,32},{32,64},{64,96},{96,128},{128,160},{160,192},{192,224},{224... | collective-permute-start | bytes 12296 | tf_op jit(solution)/shard_map/ppermute | solution.py:38
  224.9 23.1 %reduce-scatter.2.cloned.1.call-done = f32[2,2,2,16,128]{4,3,2,1,0:T(8,128)} async-done(((f32[4,2,2,16,128]{4,3,2,1,0:T(8,128)}), f32[2,2,2,16,128]{4,3,2,1,0:T(8,128)}) %reduce-scatter.2.cloned.1.call-update) | async-done | bytes 65552 | tf_op jit(solution)/shard_map/reduce_scatter | solution.py:155
  248.0 1.5 fusion.81
  250.2 2.2 fusion.33
  253.9 2.2 fusion.31
  256.1 2.2 fusion.1
  258.3 2.2 fusion
  262.3 399.2 %all-reduce.2.cloned.1.call-done = f32[2,2,2,128,128]{4,3,2,0,1:T(8,128)} async-done(((f32[2,2,2,128,128]{4,3,2,0,1:T(8,128)}), f32[2,2,2,128,128]{4,3,2,0,1:T(8,128)}) %all-reduce.2.cloned.1.call-update) | async-done | bytes 524304 | tf_op jit(solution)/shard_map/psum | solution.py:168
  (204 shorter events, 46.8 us)
Async XLA Ops:
  7.2 240.8 %reduce-scatter.2.cloned.1.call-start = ((), (), s32[]{:S(2)}) async-start(), calls=%async_computation.1 | async-start | bytes 196608 | tf_op jit(solution)/shard_map/reduce_scatter | solution.py:155
  8.2 14.4 %collective-permute-start = (f32[8,16,1]{2,1,0:T(8,128)S(1)}, f32[8,16,1]{2,1,0:T(8,128)S(1)}, u32[]{:S(2)}, u32[]{:S(2)}) collective-permute-start(f32[8,16,1]{2,1,0:T(8,128)S(1)} %bitcast.384), channel_id=1, source_target_pairs={{2,0},{4,2},{6,4},{8,6},{10,8},{12,10},{14,12},{16,14},{18,16},{20... | collective-permute-start | bytes 1544 | tf_op jit(solution)/shard_map/ppermute | solution.py:38
  14.7 10.7 %collective-permute-start.3 = (f32[8,1,128]{2,1,0:T(1,128)S(1)}, f32[8,1,128]{2,1,0:T(1,128)S(1)}, u32[]{:S(2)}, u32[]{:S(2)}) collective-permute-start(f32[8,1,128]{2,1,0:T(1,128)S(1)} %slice.631), channel_id=1, source_target_pairs={{32,0},{64,32},{96,64},{128,96},{160,128},{192,160},{224,192},{256... | collective-permute-start | bytes 12296 | tf_op jit(solution)/shard_map/ppermute | solution.py:38
  16.0 7.9 %collective-permute-start.5 = (f32[8,16,1]{2,1,0:T(8,128)S(1)}, f32[8,16,1]{2,1,0:T(8,128)S(1)}, u32[]{:S(2)}, u32[]{:S(2)}) collective-permute-start(f32[8,16,1]{2,1,0:T(8,128)S(1)} %bitcast.388), channel_id=1, source_target_pairs={{2,0},{4,2},{6,4},{8,6},{10,8},{12,10},{14,12},{16,14},{18,16},{20... | collective-permute-start | bytes 1544 | tf_op jit(solution)/shard_map/ppermute | solution.py:38
  18.0 11.3 %collective-permute-start.4 = (f32[8,1,128]{2,1,0:T(1,128)S(1)}, f32[8,1,128]{2,1,0:T(1,128)S(1)}, u32[]{:S(2)}, u32[]{:S(2)}) collective-permute-start(f32[8,1,128]{2,1,0:T(1,128)S(1)} %slice.633), channel_id=1, source_target_pairs={{32,0},{64,32},{96,64},{128,96},{160,128},{192,160},{224,192},{256... | collective-permute-start | bytes 12296 | tf_op jit(solution)/shard_map/ppermute | solution.py:38
  19.4 10.0 %collective-permute-start.1 = (f32[1,16,128]{2,1,0:T(8,128)S(1)}, f32[1,16,128]{2,1,0:T(8,128)S(1)}, u32[]{:S(2)}, u32[]{:S(2)}) collective-permute-start(f32[1,16,128]{2,1,0:T(8,128)S(1)} %get-tuple-element.102), channel_id=1, source_target_pairs={{1,0},{3,2},{5,4},{7,6},{9,8},{11,10},{13,12},{15,14},{17,16},{19,... | collective-permute-start | bytes 24584 | tf_op jit(solution)/shard_map/ppermute | solution.py:38
  22.6 6.8 %collective-permute-start.2 = (f32[1,16,128]{2,1,0:T(8,128)S(1)}, f32[1,16,128]{2,1,0:T(8,128)S(1)}, u32[]{:S(2)}, u32[]{:S(2)}) collective-permute-start(f32[1,16,128]{2,1,0:T(8,128)S(1)} %get-tuple-element.103), channel_id=1, source_target_pairs={{1,0},{3,2},{5,4},{7,6},{9,8},{11,10},{13,12},{15,14},{17,16},{19,... | collective-permute-start | bytes 24584 | tf_op jit(solution)/shard_map/ppermute | solution.py:38
  30.5 14.3 %collective-permute-start.6 = (f32[8,16,1]{2,1,0:T(8,128)S(1)}, f32[8,16,1]{2,1,0:T(8,128)S(1)}, u32[]{:S(2)}, u32[]{:S(2)}) collective-permute-start(f32[8,16,1]{2,1,0:T(8,128)S(1)} %slice.637), channel_id=1, source_target_pairs={{0,2},{2,4},{4,6},{6,8},{8,10},{10,12},{12,14},{14,16},{16,18},{18... | collective-permute-start | bytes 1544 | tf_op jit(solution)/shard_map/ppermute | solution.py:38
  34.3 10.5 %collective-permute-start.9 = (f32[8,1,128]{2,1,0:T(1,128)S(1)}, f32[8,1,128]{2,1,0:T(1,128)S(1)}, u32[]{:S(2)}, u32[]{:S(2)}) collective-permute-start(f32[8,1,128]{2,1,0:T(1,128)S(1)} %slice.645), channel_id=1, source_target_pairs={{0,32},{32,64},{64,96},{96,128},{128,160},{160,192},{192,224},{224... | collective-permute-start | bytes 12296 | tf_op jit(solution)/shard_map/ppermute | solution.py:38
  42.1 2.6 collective-permute-start.7
  43.4 2.1 collective-permute-start.8
  45.7 9.9 %collective-permute-start.11 = (f32[8,16,1]{2,1,0:T(8,128)S(1)}, f32[8,16,1]{2,1,0:T(8,128)S(1)}, u32[]{:S(2)}, u32[]{:S(2)}) collective-permute-start(f32[8,16,1]{2,1,0:T(8,128)S(1)} %slice.649), channel_id=1, source_target_pairs={{0,2},{2,4},{4,6},{6,8},{8,10},{10,12},{12,14},{14,16},{16,18},{18... | collective-permute-start | bytes 1544 | tf_op jit(solution)/shard_map/ppermute | solution.py:38
  47.8 9.1 %collective-permute-start.10 = (f32[8,1,128]{2,1,0:T(1,128)S(1)}, f32[8,1,128]{2,1,0:T(1,128)S(1)}, u32[]{:S(2)}, u32[]{:S(2)}) collective-permute-start(f32[8,1,128]{2,1,0:T(1,128)S(1)} %slice.647), channel_id=1, source_target_pairs={{0,32},{32,64},{64,96},{96,128},{128,160},{160,192},{192,224},{224... | collective-permute-start | bytes 12296 | tf_op jit(solution)/shard_map/ppermute | solution.py:38
  57.3 10.8 %collective-permute-start.12 = (f32[8,16,1]{2,1,0:T(8,128)S(1)}, f32[8,16,1]{2,1,0:T(8,128)S(1)}, u32[]{:S(2)}, u32[]{:S(2)}) collective-permute-start(f32[8,16,1]{2,1,0:T(8,128)S(1)} %bitcast.381), channel_id=1, source_target_pairs={{2,0},{4,2},{6,4},{8,6},{10,8},{12,10},{14,12},{16,14},{18,16},{20... | collective-permute-start | bytes 1544 | tf_op jit(solution)/shard_map/ppermute | solution.py:38
  63.9 9.7 %collective-permute-start.15 = (f32[8,1,128]{2,1,0:T(1,128)S(1)}, f32[8,1,128]{2,1,0:T(1,128)S(1)}, u32[]{:S(2)}, u32[]{:S(2)}) collective-permute-start(f32[8,1,128]{2,1,0:T(1,128)S(1)} %slice.661), channel_id=1, source_target_pairs={{32,0},{64,32},{96,64},{128,96},{160,128},{192,160},{224,192},{256... | collective-permute-start | bytes 12296 | tf_op jit(solution)/shard_map/ppermute | solution.py:38
  65.2 8.4 %collective-permute-start.13 = (f32[1,16,128]{2,1,0:T(8,128)S(1)}, f32[1,16,128]{2,1,0:T(8,128)S(1)}, u32[]{:S(2)}, u32[]{:S(2)}) collective-permute-start(f32[1,16,128]{2,1,0:T(8,128)S(1)} %get-tuple-element.87), channel_id=1, source_target_pairs={{1,0},{3,2},{5,4},{7,6},{9,8},{11,10},{13,12},{15,14},{17,16},{19,... | collective-permute-start | bytes 24584 | tf_op jit(solution)/shard_map/ppermute | solution.py:38
  66.5 7.1 %collective-permute-start.14 = (f32[1,16,128]{2,1,0:T(8,128)S(1)}, f32[1,16,128]{2,1,0:T(8,128)S(1)}, u32[]{:S(2)}, u32[]{:S(2)}) collective-permute-start(f32[1,16,128]{2,1,0:T(8,128)S(1)} %get-tuple-element.88), channel_id=1, source_target_pairs={{1,0},{3,2},{5,4},{7,6},{9,8},{11,10},{13,12},{15,14},{17,16},{19,... | collective-permute-start | bytes 24584 | tf_op jit(solution)/shard_map/ppermute | solution.py:38
  73.7 6.2 collective-permute-start.17
  75.9 9.7 %collective-permute-start.16 = (f32[8,1,128]{2,1,0:T(1,128)S(1)}, f32[8,1,128]{2,1,0:T(1,128)S(1)}, u32[]{:S(2)}, u32[]{:S(2)}) collective-permute-start(f32[8,1,128]{2,1,0:T(1,128)S(1)} %slice.663), channel_id=1, source_target_pairs={{32,0},{64,32},{96,64},{128,96},{160,128},{192,160},{224,192},{256... | collective-permute-start | bytes 12296 | tf_op jit(solution)/shard_map/ppermute | solution.py:38
  85.9 13.9 %collective-permute-start.18 = (f32[8,16,1]{2,1,0:T(8,128)S(1)}, f32[8,16,1]{2,1,0:T(8,128)S(1)}, u32[]{:S(2)}, u32[]{:S(2)}) collective-permute-start(f32[8,16,1]{2,1,0:T(8,128)S(1)} %slice.667), channel_id=1, source_target_pairs={{0,2},{2,4},{4,6},{6,8},{8,10},{10,12},{12,14},{14,16},{16,18},{18... | collective-permute-start | bytes 1544 | tf_op jit(solution)/shard_map/ppermute | solution.py:38
  89.3 10.5 %collective-permute-start.21 = (f32[8,1,128]{2,1,0:T(1,128)S(1)}, f32[8,1,128]{2,1,0:T(1,128)S(1)}, u32[]{:S(2)}, u32[]{:S(2)}) collective-permute-start(f32[8,1,128]{2,1,0:T(1,128)S(1)} %slice.675), channel_id=1, source_target_pairs={{0,32},{32,64},{64,96},{96,128},{128,160},{160,192},{192,224},{224... | collective-permute-start | bytes 12296 | tf_op jit(solution)/shard_map/ppermute | solution.py:38
  97.2 2.6 collective-permute-start.19
  98.4 2.1 collective-permute-start.20
  100.7 9.3 %collective-permute-start.23 = (f32[8,16,1]{2,1,0:T(8,128)S(1)}, f32[8,16,1]{2,1,0:T(8,128)S(1)}, u32[]{:S(2)}, u32[]{:S(2)}) collective-permute-start(f32[8,16,1]{2,1,0:T(8,128)S(1)} %slice.679), channel_id=1, source_target_pairs={{0,2},{2,4},{4,6},{6,8},{8,10},{10,12},{12,14},{14,16},{16,18},{18... | collective-permute-start | bytes 1544 | tf_op jit(solution)/shard_map/ppermute | solution.py:38
  102.7 8.6 %collective-permute-start.22 = (f32[8,1,128]{2,1,0:T(1,128)S(1)}, f32[8,1,128]{2,1,0:T(1,128)S(1)}, u32[]{:S(2)}, u32[]{:S(2)}) collective-permute-start(f32[8,1,128]{2,1,0:T(1,128)S(1)} %slice.677), channel_id=1, source_target_pairs={{0,32},{32,64},{64,96},{96,128},{128,160},{160,192},{192,224},{224... | collective-permute-start | bytes 12296 | tf_op jit(solution)/shard_map/ppermute | solution.py:38
  111.6 10.8 %collective-permute-start.24 = (f32[8,16,1]{2,1,0:T(8,128)S(1)}, f32[8,16,1]{2,1,0:T(8,128)S(1)}, u32[]{:S(2)}, u32[]{:S(2)}) collective-permute-start(f32[8,16,1]{2,1,0:T(8,128)S(1)} %bitcast.382), channel_id=1, source_target_pairs={{2,0},{4,2},{6,4},{8,6},{10,8},{12,10},{14,12},{16,14},{18,16},{20... | collective-permute-start | bytes 1544 | tf_op jit(solution)/shard_map/ppermute | solution.py:38
  118.2 10.2 %collective-permute-start.27 = (f32[8,1,128]{2,1,0:T(1,128)S(1)}, f32[8,1,128]{2,1,0:T(1,128)S(1)}, u32[]{:S(2)}, u32[]{:S(2)}) collective-permute-start(f32[8,1,128]{2,1,0:T(1,128)S(1)} %slice.691), channel_id=1, source_target_pairs={{32,0},{64,32},{96,64},{128,96},{160,128},{192,160},{224,192},{256... | collective-permute-start | bytes 12296 | tf_op jit(solution)/shard_map/ppermute | solution.py:38
  119.5 8.9 %collective-permute-start.25 = (f32[1,16,128]{2,1,0:T(8,128)S(1)}, f32[1,16,128]{2,1,0:T(8,128)S(1)}, u32[]{:S(2)}, u32[]{:S(2)}) collective-permute-start(f32[1,16,128]{2,1,0:T(8,128)S(1)} %get-tuple-element.71), channel_id=1, source_target_pairs={{1,0},{3,2},{5,4},{7,6},{9,8},{11,10},{13,12},{15,14},{17,16},{19,... | collective-permute-start | bytes 24584 | tf_op jit(solution)/shard_map/ppermute | solution.py:38
  120.8 7.6 %collective-permute-start.26 = (f32[1,16,128]{2,1,0:T(8,128)S(1)}, f32[1,16,128]{2,1,0:T(8,128)S(1)}, u32[]{:S(2)}, u32[]{:S(2)}) collective-permute-start(f32[1,16,128]{2,1,0:T(8,128)S(1)} %get-tuple-element.72), channel_id=1, source_target_pairs={{1,0},{3,2},{5,4},{7,6},{9,8},{11,10},{13,12},{15,14},{17,16},{19,... | collective-permute-start | bytes 24584 | tf_op jit(solution)/shard_map/ppermute | solution.py:38
  128.6 6.2 collective-permute-start.29
  131.6 9.7 %collective-permute-start.28 = (f32[8,1,128]{2,1,0:T(1,128)S(1)}, f32[8,1,128]{2,1,0:T(1,128)S(1)}, u32[]{:S(2)}, u32[]{:S(2)}) collective-permute-start(f32[8,1,128]{2,1,0:T(1,128)S(1)} %slice.693), channel_id=1, source_target_pairs={{32,0},{64,32},{96,64},{128,96},{160,128},{192,160},{224,192},{256... | collective-permute-start | bytes 12296 | tf_op jit(solution)/shard_map/ppermute | solution.py:38
  141.6 13.3 %collective-permute-start.30 = (f32[8,16,1]{2,1,0:T(8,128)S(1)}, f32[8,16,1]{2,1,0:T(8,128)S(1)}, u32[]{:S(2)}, u32[]{:S(2)}) collective-permute-start(f32[8,16,1]{2,1,0:T(8,128)S(1)} %slice.697), channel_id=1, source_target_pairs={{0,2},{2,4},{4,6},{6,8},{8,10},{10,12},{12,14},{14,16},{16,18},{18... | collective-permute-start | bytes 1544 | tf_op jit(solution)/shard_map/ppermute | solution.py:38
  144.5 10.5 %collective-permute-start.33 = (f32[8,1,128]{2,1,0:T(1,128)S(1)}, f32[8,1,128]{2,1,0:T(1,128)S(1)}, u32[]{:S(2)}, u32[]{:S(2)}) collective-permute-start(f32[8,1,128]{2,1,0:T(1,128)S(1)} %slice.705), channel_id=1, source_target_pairs={{0,32},{32,64},{64,96},{96,128},{128,160},{160,192},{192,224},{224... | collective-permute-start | bytes 12296 | tf_op jit(solution)/shard_map/ppermute | solution.py:38
  152.3 2.6 collective-permute-start.31
  155.9 9.8 %collective-permute-start.35 = (f32[8,16,1]{2,1,0:T(8,128)S(1)}, f32[8,16,1]{2,1,0:T(8,128)S(1)}, u32[]{:S(2)}, u32[]{:S(2)}) collective-permute-start(f32[8,16,1]{2,1,0:T(8,128)S(1)} %slice.709), channel_id=1, source_target_pairs={{0,2},{2,4},{4,6},{6,8},{8,10},{10,12},{12,14},{14,16},{16,18},{18... | collective-permute-start | bytes 1544 | tf_op jit(solution)/shard_map/ppermute | solution.py:38
  157.9 9.1 %collective-permute-start.34 = (f32[8,1,128]{2,1,0:T(1,128)S(1)}, f32[8,1,128]{2,1,0:T(1,128)S(1)}, u32[]{:S(2)}, u32[]{:S(2)}) collective-permute-start(f32[8,1,128]{2,1,0:T(1,128)S(1)} %slice.707), channel_id=1, source_target_pairs={{0,32},{32,64},{64,96},{96,128},{128,160},{160,192},{192,224},{224... | collective-permute-start | bytes 12296 | tf_op jit(solution)/shard_map/ppermute | solution.py:38
  167.4 10.8 %collective-permute-start.36 = (f32[8,16,1]{2,1,0:T(8,128)S(1)}, f32[8,16,1]{2,1,0:T(8,128)S(1)}, u32[]{:S(2)}, u32[]{:S(2)}) collective-permute-start(f32[8,16,1]{2,1,0:T(8,128)S(1)} %bitcast.383), channel_id=1, source_target_pairs={{2,0},{4,2},{6,4},{8,6},{10,8},{12,10},{14,12},{16,14},{18,16},{20... | collective-permute-start | bytes 1544 | tf_op jit(solution)/shard_map/ppermute | solution.py:38
  174.1 9.7 %collective-permute-start.39 = (f32[8,1,128]{2,1,0:T(1,128)S(1)}, f32[8,1,128]{2,1,0:T(1,128)S(1)}, u32[]{:S(2)}, u32[]{:S(2)}) collective-permute-start(f32[8,1,128]{2,1,0:T(1,128)S(1)} %slice.721), channel_id=1, source_target_pairs={{32,0},{64,32},{96,64},{128,96},{160,128},{192,160},{224,192},{256... | collective-permute-start | bytes 12296 | tf_op jit(solution)/shard_map/ppermute | solution.py:38
  175.4 8.4 %collective-permute-start.37 = (f32[1,16,128]{2,1,0:T(8,128)S(1)}, f32[1,16,128]{2,1,0:T(8,128)S(1)}, u32[]{:S(2)}, u32[]{:S(2)}) collective-permute-start(f32[1,16,128]{2,1,0:T(8,128)S(1)} %get-tuple-element.55), channel_id=1, source_target_pairs={{1,0},{3,2},{5,4},{7,6},{9,8},{11,10},{13,12},{15,14},{17,16},{19,... | collective-permute-start | bytes 24584 | tf_op jit(solution)/shard_map/ppermute | solution.py:38
  176.7 7.1 %collective-permute-start.38 = (f32[1,16,128]{2,1,0:T(8,128)S(1)}, f32[1,16,128]{2,1,0:T(8,128)S(1)}, u32[]{:S(2)}, u32[]{:S(2)}) collective-permute-start(f32[1,16,128]{2,1,0:T(8,128)S(1)} %get-tuple-element.56), channel_id=1, source_target_pairs={{1,0},{3,2},{5,4},{7,6},{9,8},{11,10},{13,12},{15,14},{17,16},{19,... | collective-permute-start | bytes 24584 | tf_op jit(solution)/shard_map/ppermute | solution.py:38
  183.9 6.2 collective-permute-start.41
  186.9 9.4 %collective-permute-start.40 = (f32[8,1,128]{2,1,0:T(1,128)S(1)}, f32[8,1,128]{2,1,0:T(1,128)S(1)}, u32[]{:S(2)}, u32[]{:S(2)}) collective-permute-start(f32[8,1,128]{2,1,0:T(1,128)S(1)} %slice.723), channel_id=1, source_target_pairs={{32,0},{64,32},{96,64},{128,96},{160,128},{192,160},{224,192},{256... | collective-permute-start | bytes 12296 | tf_op jit(solution)/shard_map/ppermute | solution.py:38
  196.6 13.3 %collective-permute-start.42 = (f32[8,16,1]{2,1,0:T(8,128)S(1)}, f32[8,16,1]{2,1,0:T(8,128)S(1)}, u32[]{:S(2)}, u32[]{:S(2)}) collective-permute-start(f32[8,16,1]{2,1,0:T(8,128)S(1)} %slice.727), channel_id=1, source_target_pairs={{0,2},{2,4},{4,6},{6,8},{8,10},{10,12},{12,14},{14,16},{16,18},{18... | collective-permute-start | bytes 1544 | tf_op jit(solution)/shard_map/ppermute | solution.py:38
  199.5 10.5 %collective-permute-start.45 = (f32[8,1,128]{2,1,0:T(1,128)S(1)}, f32[8,1,128]{2,1,0:T(1,128)S(1)}, u32[]{:S(2)}, u32[]{:S(2)}) collective-permute-start(f32[8,1,128]{2,1,0:T(1,128)S(1)} %slice.735), channel_id=1, source_target_pairs={{0,32},{32,64},{64,96},{96,128},{128,160},{160,192},{192,224},{224... | collective-permute-start | bytes 12296 | tf_op jit(solution)/shard_map/ppermute | solution.py:38
  207.4 2.6 collective-permute-start.43
  211.0 9.8 %collective-permute-start.47 = (f32[8,16,1]{2,1,0:T(8,128)S(1)}, f32[8,16,1]{2,1,0:T(8,128)S(1)}, u32[]{:S(2)}, u32[]{:S(2)}) collective-permute-start(f32[8,16,1]{2,1,0:T(8,128)S(1)} %slice.739), channel_id=1, source_target_pairs={{0,2},{2,4},{4,6},{6,8},{8,10},{10,12},{12,14},{14,16},{16,18},{18... | collective-permute-start | bytes 1544 | tf_op jit(solution)/shard_map/ppermute | solution.py:38
  212.9 9.1 %collective-permute-start.46 = (f32[8,1,128]{2,1,0:T(1,128)S(1)}, f32[8,1,128]{2,1,0:T(1,128)S(1)}, u32[]{:S(2)}, u32[]{:S(2)}) collective-permute-start(f32[8,1,128]{2,1,0:T(1,128)S(1)} %slice.737), channel_id=1, source_target_pairs={{0,32},{32,64},{64,96},{96,128},{128,160},{160,192},{192,224},{224... | collective-permute-start | bytes 12296 | tf_op jit(solution)/shard_map/ppermute | solution.py:38
  224.6 437.0 %all-reduce.2.cloned.1.call-start = ((), (), s32[]{:S(2)}) async-start(), calls=%async_computation.2 | async-start | bytes 1048576 | tf_op jit(solution)/shard_map/psum | solution.py:168
  (9 other events, 57.3 us)
Sparse Core Ops, SparseCore 0:
  224.7 23.2 reduce-scatter.1
  261.5 399.9 all-reduce.1
where the time goes:
time: 671 us; the launch traced here: 670 us
  waiting for transfers between devices  478 us (71%)
  starting transfers between devices  151 us (23%)
  between operations  16.1 us (2%)
  matrix products  14.1 us (2%)
  local copies, waits for them, and re-layouts  6.84 us (1%)
    psum x1, waiting for transfers between devices, body(): total = lax.psum(jnp.stack([far_re, far_im], 1), ('mx', 'my'))  399 us
    ppermute x48, starting transfers between devices, from_behind(): return lax.ppermute(x, axis, pairs)  150 us
    ppermute x48, waiting for transfers between devices, from_behind(): return lax.ppermute(x, axis, pairs)  55.5 us
    reduce_scatter x1, waiting for transfers between devices, body(): mine = lax.psum_scatter(phasor, 'dz', scatter_dimension=0, tiled=True)  23.1 us
    dot_general x14, matrix products, product_of(): return jnp.einsum(form, left, right, precision=lax.Precision.HIGHEST)  14.1 us
  transfers between devices with their start and end apart: 50, of which 21 were waited for; matrix products, arithmetic and copies ran while one was open for 0% of the time, Pallas kernels for 0%

commit v1 on v0

--- a/solution.py
+++ b/solution.py
@@ -165,7 +165,7 @@
     rows_share = U // lax.axis_size("mx")
     cols_share = V // lax.axis_size("my")
     far_re, far_im = along_columns(mid_re, mid_im, col_re, col_im)
-    total = lax.psum(jnp.stack([far_re, far_im], 1), ("mx", "my"))
+    total = lax.psum(lax.psum(jnp.stack([far_re, far_im], 1), "mx"), "my")
     total = lax.dynamic_slice_in_dim(total, lax.axis_index("mx") * rows_share, rows_share, 3)
     far_field = lax.dynamic_slice_in_dim(total, lax.axis_index("my") * cols_share, cols_share, 4)
     poles_next = jnp.stack([polar, current, drude])

time: 671 us -> 650 us (0.969)
  the two profiles are of different devices: /device:TPU:4 before, /device:TPU:8 now
where the time goes in v1:
time: 650 us; the launch traced here: 649 us
  waiting for transfers between devices  461 us (71%)
  starting transfers between devices  147 us (23%)
  between operations  15.8 us (2%)
  matrix products  14.1 us (2%)
  local copies, waits for them, and re-layouts  6.85 us (1%)
    psum x2, waiting for transfers between devices, body(): total = lax.psum(lax.psum(jnp.stack([far_re, far_im], 1), 'mx'), 'my')  378 us
    ppermute x48, starting transfers between devices, from_behind(): return lax.ppermute(x, axis, pairs)  146 us
    ppermute x48, waiting for transfers between devices, from_behind(): return lax.ppermute(x, axis, pairs)  66.7 us
    reduce_scatter x1, waiting for transfers between devices, body(): mine = lax.psum_scatter(phasor, 'dz', scatter_dimension=0, tiled=True)  16 us
    dot_general x14, matrix products, product_of(): return jnp.einsum(form, left, right, precision=lax.Precision.HIGHEST)  14.1 us
  transfers between devices with their start and end apart: 51, of which 21 were waited for; matrix products, arithmetic and copies ran while one was open for 0% of the time, Pallas kernels for 0%

profile of v1, /device:TPU:8, one launch (start us, length us, event | category | flops | bytes accessed | tf_op | source)
XLA Modules:
  0.0 648.9 jit_solution(13905828841242878273)
XLA Ops:
  9.5 12.6 %collective-permute-start.3 = (f32[8,1,128]{2,1,0:T(1,128)S(1)}, f32[8,1,128]{2,1,0:T(1,128)S(1)}, u32[]{:S(2)}, u32[]{:S(2)}) collective-permute-start(f32[8,1,128]{2,1,0:T(1,128)S(1)} %slice.631), channel_id=1, source_target_pairs={{32,0},{64,32},{96,64},{128,96},{160,128},{192,160},{224,192},{256... | collective-permute-start | bytes 12296 | tf_op jit(solution)/shard_map/ppermute | solution.py:38
  23.4 5.5 collective-permute-start.4
  33.5 1.7 collective-permute-done.2
  36.3 5.2 collective-permute-start.6
  41.5 4.3 collective-permute-start.9
  45.8 1.5 collective-permute-start.7
  48.6 3.2 collective-permute-done.9
  52.0 4.1 collective-permute-start.11
  56.1 3.4 collective-permute-start.10
  59.5 6.9 %collective-permute-done.10 = f32[8,1,128]{2,1,0:T(1,128)S(1)} collective-permute-done((f32[8,1,128]{2,1,0:T(1,128)S(1)}, f32[8,1,128]{2,1,0:T(1,128)S(1)}, u32[]{:S(2)}, u32[]{:S(2)}) %collective-permute-start.10) | collective-permute-done | bytes 4128 | tf_op jit(solution)/shard_map/ppermute | solution.py:38
  68.0 3.1 collective-permute-start.15
  74.0 3.4 collective-permute-done.15
  78.9 4.0 collective-permute-start.16
  84.4 3.9 collective-permute-done.16
  88.6 5.2 collective-permute-start.18
  93.8 4.7 collective-permute-start.21
  101.1 3.0 collective-permute-done.21
  104.3 4.6 collective-permute-start.23
  108.9 3.8 collective-permute-start.22
  112.8 6.5 collective-permute-done.22
  120.8 3.1 collective-permute-start.27
  126.9 3.4 collective-permute-done.27
  131.7 4.0 collective-permute-start.28
  137.2 4.0 collective-permute-done.28
  141.6 5.1 collective-permute-start.30
  146.7 4.7 collective-permute-start.33
  154.0 3.0 collective-permute-done.33
  157.2 6.6 %collective-permute-start.35 = (f32[8,16,1]{2,1,0:T(8,128)S(1)}, f32[8,16,1]{2,1,0:T(8,128)S(1)}, u32[]{:S(2)}, u32[]{:S(2)}) collective-permute-start(f32[8,16,1]{2,1,0:T(8,128)S(1)} %slice.709), channel_id=1, source_target_pairs={{0,2},{2,4},{4,6},{6,8},{8,10},{10,12},{12,14},{14,16},{16,18},{18... | collective-permute-start | bytes 1544 | tf_op jit(solution)/shard_map/ppermute | solution.py:38
  163.8 3.8 collective-permute-start.34
  167.6 6.5 collective-permute-done.34
  175.8 3.1 collective-permute-start.39
  181.9 3.4 collective-permute-done.39
  186.7 4.0 collective-permute-start.40
  192.2 4.0 collective-permute-done.40
  196.6 5.1 collective-permute-start.42
  201.7 4.7 collective-permute-start.45
  209.0 3.0 collective-permute-done.45
  212.2 6.6 %collective-permute-start.47 = (f32[8,16,1]{2,1,0:T(8,128)S(1)}, f32[8,16,1]{2,1,0:T(8,128)S(1)}, u32[]{:S(2)}, u32[]{:S(2)}) collective-permute-start(f32[8,16,1]{2,1,0:T(8,128)S(1)} %slice.739), channel_id=1, source_target_pairs={{0,2},{2,4},{4,6},{6,8},{8,10},{10,12},{12,14},{14,16},{16,18},{18... | collective-permute-start | bytes 1544 | tf_op jit(solution)/shard_map/ppermute | solution.py:38
  218.8 3.8 collective-permute-start.46
  222.7 6.5 collective-permute-done.46
  232.0 16.0 %reduce-scatter.2.cloned.1.call-done = f32[2,2,2,16,128]{4,3,2,1,0:T(8,128)} async-done(((f32[4,2,2,16,128]{4,3,2,1,0:T(8,128)}), f32[2,2,2,16,128]{4,3,2,1,0:T(8,128)}) %reduce-scatter.2.cloned.1.call-update) | async-done | bytes 65552 | tf_op jit(solution)/shard_map/reduce_scatter | solution.py:155
  247.9 1.5 fusion.81
  250.2 2.2 fusion.33
  253.9 2.2 fusion.31
  256.1 2.2 fusion.1
  258.3 2.2 fusion
  261.4 207.1 %all-reduce.3.cloned.1.call-done = f32[2,2,2,128,128]{4,3,2,0,1:T(8,128)} async-done(((f32[2,2,2,128,128]{4,3,2,0,1:T(8,128)}), f32[2,2,2,128,128]{4,3,2,0,1:T(8,128)}) %all-reduce.3.cloned.1.call-update) | async-done | bytes 524304 | tf_op jit(solution)/shard_map/psum | solution.py:168
  469.4 171.3 %all-reduce.5.cloned.1.call-done = f32[2,2,2,128,128]{4,3,2,0,1:T(8,128)} async-done(((f32[2,2,2,128,128]{4,3,2,0,1:T(8,128)}), f32[2,2,2,128,128]{4,3,2,0,1:T(8,128)}) %all-reduce.5.cloned.1.call-update) | async-done | bytes 524304 | tf_op jit(solution)/shard_map/psum | solution.py:168
  (207 shorter events, 49.6 us)
Async XLA Ops:
  7.2 240.8 %reduce-scatter.2.cloned.1.call-start = ((), (), s32[]{:S(2)}) async-start(), calls=%async_computation.1 | async-start | bytes 196608 | tf_op jit(solution)/shard_map/reduce_scatter | solution.py:155
  8.2 23.9 %collective-permute-start = (f32[8,16,1]{2,1,0:T(8,128)S(1)}, f32[8,16,1]{2,1,0:T(8,128)S(1)}, u32[]{:S(2)}, u32[]{:S(2)}) collective-permute-start(f32[8,16,1]{2,1,0:T(8,128)S(1)} %bitcast.384), channel_id=1, source_target_pairs={{2,0},{4,2},{6,4},{8,6},{10,8},{12,10},{14,12},{16,14},{18,16},{20... | collective-permute-start | bytes 1544 | tf_op jit(solution)/shard_map/ppermute | solution.py:38
  9.5 24.0 %collective-permute-start.3 = (f32[8,1,128]{2,1,0:T(1,128)S(1)}, f32[8,1,128]{2,1,0:T(1,128)S(1)}, u32[]{:S(2)}, u32[]{:S(2)}) collective-permute-start(f32[8,1,128]{2,1,0:T(1,128)S(1)} %slice.631), channel_id=1, source_target_pairs={{32,0},{64,32},{96,64},{128,96},{160,128},{192,160},{224,192},{256... | collective-permute-start | bytes 12296 | tf_op jit(solution)/shard_map/ppermute | solution.py:38
  22.1 11.3 %collective-permute-start.5 = (f32[8,16,1]{2,1,0:T(8,128)S(1)}, f32[8,16,1]{2,1,0:T(8,128)S(1)}, u32[]{:S(2)}, u32[]{:S(2)}) collective-permute-start(f32[8,16,1]{2,1,0:T(8,128)S(1)} %bitcast.388), channel_id=1, source_target_pairs={{2,0},{4,2},{6,4},{8,6},{10,8},{12,10},{14,12},{16,14},{18,16},{20... | collective-permute-start | bytes 1544 | tf_op jit(solution)/shard_map/ppermute | solution.py:38
  23.4 10.0 %collective-permute-start.4 = (f32[8,1,128]{2,1,0:T(1,128)S(1)}, f32[8,1,128]{2,1,0:T(1,128)S(1)}, u32[]{:S(2)}, u32[]{:S(2)}) collective-permute-start(f32[8,1,128]{2,1,0:T(1,128)S(1)} %slice.633), channel_id=1, source_target_pairs={{32,0},{64,32},{96,64},{128,96},{160,128},{192,160},{224,192},{256... | collective-permute-start | bytes 12296 | tf_op jit(solution)/shard_map/ppermute | solution.py:38
  28.9 4.5 collective-permute-start.1
  36.3 12.3 %collective-permute-start.6 = (f32[8,16,1]{2,1,0:T(8,128)S(1)}, f32[8,16,1]{2,1,0:T(8,128)S(1)}, u32[]{:S(2)}, u32[]{:S(2)}) collective-permute-start(f32[8,16,1]{2,1,0:T(8,128)S(1)} %slice.637), channel_id=1, source_target_pairs={{0,2},{2,4},{4,6},{6,8},{8,10},{10,12},{12,14},{14,16},{16,18},{18... | collective-permute-start | bytes 1544 | tf_op jit(solution)/shard_map/ppermute | solution.py:38
  41.5 10.3 %collective-permute-start.9 = (f32[8,1,128]{2,1,0:T(1,128)S(1)}, f32[8,1,128]{2,1,0:T(1,128)S(1)}, u32[]{:S(2)}, u32[]{:S(2)}) collective-permute-start(f32[8,1,128]{2,1,0:T(1,128)S(1)} %slice.645), channel_id=1, source_target_pairs={{0,32},{32,64},{64,96},{96,128},{128,160},{160,192},{192,224},{224... | collective-permute-start | bytes 12296 | tf_op jit(solution)/shard_map/ppermute | solution.py:38
  45.8 6.0 collective-permute-start.7
  47.3 4.5 collective-permute-start.8
  52.0 7.5 %collective-permute-start.11 = (f32[8,16,1]{2,1,0:T(8,128)S(1)}, f32[8,16,1]{2,1,0:T(8,128)S(1)}, u32[]{:S(2)}, u32[]{:S(2)}) collective-permute-start(f32[8,16,1]{2,1,0:T(8,128)S(1)} %slice.649), channel_id=1, source_target_pairs={{0,2},{2,4},{4,6},{6,8},{8,10},{10,12},{12,14},{14,16},{16,18},{18... | collective-permute-start | bytes 1544 | tf_op jit(solution)/shard_map/ppermute | solution.py:38
  56.1 10.3 %collective-permute-start.10 = (f32[8,1,128]{2,1,0:T(1,128)S(1)}, f32[8,1,128]{2,1,0:T(1,128)S(1)}, u32[]{:S(2)}, u32[]{:S(2)}) collective-permute-start(f32[8,1,128]{2,1,0:T(1,128)S(1)} %slice.647), channel_id=1, source_target_pairs={{0,32},{32,64},{64,96},{96,128},{128,160},{160,192},{192,224},{224... | collective-permute-start | bytes 12296 | tf_op jit(solution)/shard_map/ppermute | solution.py:38
  66.7 7.3 %collective-permute-start.12 = (f32[8,16,1]{2,1,0:T(8,128)S(1)}, f32[8,16,1]{2,1,0:T(8,128)S(1)}, u32[]{:S(2)}, u32[]{:S(2)}) collective-permute-start(f32[8,16,1]{2,1,0:T(8,128)S(1)} %bitcast.381), channel_id=1, source_target_pairs={{2,0},{4,2},{6,4},{8,6},{10,8},{12,10},{14,12},{16,14},{18,16},{20... | collective-permute-start | bytes 1544 | tf_op jit(solution)/shard_map/ppermute | solution.py:38
  68.0 9.4 %collective-permute-start.15 = (f32[8,1,128]{2,1,0:T(1,128)S(1)}, f32[8,1,128]{2,1,0:T(1,128)S(1)}, u32[]{:S(2)}, u32[]{:S(2)}) collective-permute-start(f32[8,1,128]{2,1,0:T(1,128)S(1)} %slice.661), channel_id=1, source_target_pairs={{32,0},{64,32},{96,64},{128,96},{160,128},{192,160},{224,192},{256... | collective-permute-start | bytes 12296 | tf_op jit(solution)/shard_map/ppermute | solution.py:38
  71.1 6.3 collective-permute-start.13
  72.4 5.0 collective-permute-start.14
  77.6 6.8 %collective-permute-start.17 = (f32[8,16,1]{2,1,0:T(8,128)S(1)}, f32[8,16,1]{2,1,0:T(8,128)S(1)}, u32[]{:S(2)}, u32[]{:S(2)}) collective-permute-start(f32[8,16,1]{2,1,0:T(8,128)S(1)} %bitcast.385), channel_id=1, source_target_pairs={{2,0},{4,2},{6,4},{8,6},{10,8},{12,10},{14,12},{16,14},{18,16},{20... | collective-permute-start | bytes 1544 | tf_op jit(solution)/shard_map/ppermute | solution.py:38
  78.9 9.4 %collective-permute-start.16 = (f32[8,1,128]{2,1,0:T(1,128)S(1)}, f32[8,1,128]{2,1,0:T(1,128)S(1)}, u32[]{:S(2)}, u32[]{:S(2)}) collective-permute-start(f32[8,1,128]{2,1,0:T(1,128)S(1)} %slice.663), channel_id=1, source_target_pairs={{32,0},{64,32},{96,64},{128,96},{160,128},{192,160},{224,192},{256... | collective-permute-start | bytes 12296 | tf_op jit(solution)/shard_map/ppermute | solution.py:38
  88.6 12.5 %collective-permute-start.18 = (f32[8,16,1]{2,1,0:T(8,128)S(1)}, f32[8,16,1]{2,1,0:T(8,128)S(1)}, u32[]{:S(2)}, u32[]{:S(2)}) collective-permute-start(f32[8,16,1]{2,1,0:T(8,128)S(1)} %slice.667), channel_id=1, source_target_pairs={{0,2},{2,4},{4,6},{6,8},{8,10},{10,12},{12,14},{14,16},{16,18},{18... | collective-permute-start | bytes 1544 | tf_op jit(solution)/shard_map/ppermute | solution.py:38
  93.8 10.3 %collective-permute-start.21 = (f32[8,1,128]{2,1,0:T(1,128)S(1)}, f32[8,1,128]{2,1,0:T(1,128)S(1)}, u32[]{:S(2)}, u32[]{:S(2)}) collective-permute-start(f32[8,1,128]{2,1,0:T(1,128)S(1)} %slice.675), channel_id=1, source_target_pairs={{0,32},{32,64},{64,96},{96,128},{128,160},{160,192},{192,224},{224... | collective-permute-start | bytes 12296 | tf_op jit(solution)/shard_map/ppermute | solution.py:38
  98.5 5.6 collective-permute-start.19
  104.3 8.5 %collective-permute-start.23 = (f32[8,16,1]{2,1,0:T(8,128)S(1)}, f32[8,16,1]{2,1,0:T(8,128)S(1)}, u32[]{:S(2)}, u32[]{:S(2)}) collective-permute-start(f32[8,16,1]{2,1,0:T(8,128)S(1)} %slice.679), channel_id=1, source_target_pairs={{0,2},{2,4},{4,6},{6,8},{8,10},{10,12},{12,14},{14,16},{16,18},{18... | collective-permute-start | bytes 1544 | tf_op jit(solution)/shard_map/ppermute | solution.py:38
  108.9 10.3 %collective-permute-start.22 = (f32[8,1,128]{2,1,0:T(1,128)S(1)}, f32[8,1,128]{2,1,0:T(1,128)S(1)}, u32[]{:S(2)}, u32[]{:S(2)}) collective-permute-start(f32[8,1,128]{2,1,0:T(1,128)S(1)} %slice.677), channel_id=1, source_target_pairs={{0,32},{32,64},{64,96},{96,128},{128,160},{160,192},{192,224},{224... | collective-permute-start | bytes 12296 | tf_op jit(solution)/shard_map/ppermute | solution.py:38
  119.5 7.3 %collective-permute-start.24 = (f32[8,16,1]{2,1,0:T(8,128)S(1)}, f32[8,16,1]{2,1,0:T(8,128)S(1)}, u32[]{:S(2)}, u32[]{:S(2)}) collective-permute-start(f32[8,16,1]{2,1,0:T(8,128)S(1)} %bitcast.382), channel_id=1, source_target_pairs={{2,0},{4,2},{6,4},{8,6},{10,8},{12,10},{14,12},{16,14},{18,16},{20... | collective-permute-start | bytes 1544 | tf_op jit(solution)/shard_map/ppermute | solution.py:38
  120.8 9.4 %collective-permute-start.27 = (f32[8,1,128]{2,1,0:T(1,128)S(1)}, f32[8,1,128]{2,1,0:T(1,128)S(1)}, u32[]{:S(2)}, u32[]{:S(2)}) collective-permute-start(f32[8,1,128]{2,1,0:T(1,128)S(1)} %slice.691), channel_id=1, source_target_pairs={{32,0},{64,32},{96,64},{128,96},{160,128},{192,160},{224,192},{256... | collective-permute-start | bytes 12296 | tf_op jit(solution)/shard_map/ppermute | solution.py:38
  124.0 6.3 collective-permute-start.25
  125.3 5.0 collective-permute-start.26
  130.4 6.8 %collective-permute-start.29 = (f32[8,16,1]{2,1,0:T(8,128)S(1)}, f32[8,16,1]{2,1,0:T(8,128)S(1)}, u32[]{:S(2)}, u32[]{:S(2)}) collective-permute-start(f32[8,16,1]{2,1,0:T(8,128)S(1)} %bitcast.386), channel_id=1, source_target_pairs={{2,0},{4,2},{6,4},{8,6},{10,8},{12,10},{14,12},{16,14},{18,16},{20... | collective-permute-start | bytes 1544 | tf_op jit(solution)/shard_map/ppermute | solution.py:38
  131.7 9.5 %collective-permute-start.28 = (f32[8,1,128]{2,1,0:T(1,128)S(1)}, f32[8,1,128]{2,1,0:T(1,128)S(1)}, u32[]{:S(2)}, u32[]{:S(2)}) collective-permute-start(f32[8,1,128]{2,1,0:T(1,128)S(1)} %slice.693), channel_id=1, source_target_pairs={{32,0},{64,32},{96,64},{128,96},{160,128},{192,160},{224,192},{256... | collective-permute-start | bytes 12296 | tf_op jit(solution)/shard_map/ppermute | solution.py:38
  141.6 12.4 %collective-permute-start.30 = (f32[8,16,1]{2,1,0:T(8,128)S(1)}, f32[8,16,1]{2,1,0:T(8,128)S(1)}, u32[]{:S(2)}, u32[]{:S(2)}) collective-permute-start(f32[8,16,1]{2,1,0:T(8,128)S(1)} %slice.697), channel_id=1, source_target_pairs={{0,2},{2,4},{4,6},{6,8},{8,10},{10,12},{12,14},{14,16},{16,18},{18... | collective-permute-start | bytes 1544 | tf_op jit(solution)/shard_map/ppermute | solution.py:38
  146.7 10.3 %collective-permute-start.33 = (f32[8,1,128]{2,1,0:T(1,128)S(1)}, f32[8,1,128]{2,1,0:T(1,128)S(1)}, u32[]{:S(2)}, u32[]{:S(2)}) collective-permute-start(f32[8,1,128]{2,1,0:T(1,128)S(1)} %slice.705), channel_id=1, source_target_pairs={{0,32},{32,64},{64,96},{96,128},{128,160},{160,192},{192,224},{224... | collective-permute-start | bytes 12296 | tf_op jit(solution)/shard_map/ppermute | solution.py:38
  151.4 5.6 collective-permute-start.31
  157.2 10.5 %collective-permute-start.35 = (f32[8,16,1]{2,1,0:T(8,128)S(1)}, f32[8,16,1]{2,1,0:T(8,128)S(1)}, u32[]{:S(2)}, u32[]{:S(2)}) collective-permute-start(f32[8,16,1]{2,1,0:T(8,128)S(1)} %slice.709), channel_id=1, source_target_pairs={{0,2},{2,4},{4,6},{6,8},{8,10},{10,12},{12,14},{14,16},{16,18},{18... | collective-permute-start | bytes 1544 | tf_op jit(solution)/shard_map/ppermute | solution.py:38
  163.8 10.3 %collective-permute-start.34 = (f32[8,1,128]{2,1,0:T(1,128)S(1)}, f32[8,1,128]{2,1,0:T(1,128)S(1)}, u32[]{:S(2)}, u32[]{:S(2)}) collective-permute-start(f32[8,1,128]{2,1,0:T(1,128)S(1)} %slice.707), channel_id=1, source_target_pairs={{0,32},{32,64},{64,96},{96,128},{128,160},{160,192},{192,224},{224... | collective-permute-start | bytes 12296 | tf_op jit(solution)/shard_map/ppermute | solution.py:38
  174.5 7.3 %collective-permute-start.36 = (f32[8,16,1]{2,1,0:T(8,128)S(1)}, f32[8,16,1]{2,1,0:T(8,128)S(1)}, u32[]{:S(2)}, u32[]{:S(2)}) collective-permute-start(f32[8,16,1]{2,1,0:T(8,128)S(1)} %bitcast.383), channel_id=1, source_target_pairs={{2,0},{4,2},{6,4},{8,6},{10,8},{12,10},{14,12},{16,14},{18,16},{20... | collective-permute-start | bytes 1544 | tf_op jit(solution)/shard_map/ppermute | solution.py:38
  175.8 9.4 %collective-permute-start.39 = (f32[8,1,128]{2,1,0:T(1,128)S(1)}, f32[8,1,128]{2,1,0:T(1,128)S(1)}, u32[]{:S(2)}, u32[]{:S(2)}) collective-permute-start(f32[8,1,128]{2,1,0:T(1,128)S(1)} %slice.721), channel_id=1, source_target_pairs={{32,0},{64,32},{96,64},{128,96},{160,128},{192,160},{224,192},{256... | collective-permute-start | bytes 12296 | tf_op jit(solution)/shard_map/ppermute | solution.py:38
  179.0 6.3 collective-permute-start.37
  180.3 5.0 collective-permute-start.38
  185.4 6.8 %collective-permute-start.41 = (f32[8,16,1]{2,1,0:T(8,128)S(1)}, f32[8,16,1]{2,1,0:T(8,128)S(1)}, u32[]{:S(2)}, u32[]{:S(2)}) collective-permute-start(f32[8,16,1]{2,1,0:T(8,128)S(1)} %bitcast.387), channel_id=1, source_target_pairs={{2,0},{4,2},{6,4},{8,6},{10,8},{12,10},{14,12},{16,14},{18,16},{20... | collective-permute-start | bytes 1544 | tf_op jit(solution)/shard_map/ppermute | solution.py:38
  186.7 9.5 %collective-permute-start.40 = (f32[8,1,128]{2,1,0:T(1,128)S(1)}, f32[8,1,128]{2,1,0:T(1,128)S(1)}, u32[]{:S(2)}, u32[]{:S(2)}) collective-permute-start(f32[8,1,128]{2,1,0:T(1,128)S(1)} %slice.723), channel_id=1, source_target_pairs={{32,0},{64,32},{96,64},{128,96},{160,128},{192,160},{224,192},{256... | collective-permute-start | bytes 12296 | tf_op jit(solution)/shard_map/ppermute | solution.py:38
  196.6 12.4 %collective-permute-start.42 = (f32[8,16,1]{2,1,0:T(8,128)S(1)}, f32[8,16,1]{2,1,0:T(8,128)S(1)}, u32[]{:S(2)}, u32[]{:S(2)}) collective-permute-start(f32[8,16,1]{2,1,0:T(8,128)S(1)} %slice.727), channel_id=1, source_target_pairs={{0,2},{2,4},{4,6},{6,8},{8,10},{10,12},{12,14},{14,16},{16,18},{18... | collective-permute-start | bytes 1544 | tf_op jit(solution)/shard_map/ppermute | solution.py:38
  201.7 10.3 %collective-permute-start.45 = (f32[8,1,128]{2,1,0:T(1,128)S(1)}, f32[8,1,128]{2,1,0:T(1,128)S(1)}, u32[]{:S(2)}, u32[]{:S(2)}) collective-permute-start(f32[8,1,128]{2,1,0:T(1,128)S(1)} %slice.735), channel_id=1, source_target_pairs={{0,32},{32,64},{64,96},{96,128},{128,160},{160,192},{192,224},{224... | collective-permute-start | bytes 12296 | tf_op jit(solution)/shard_map/ppermute | solution.py:38
  206.4 5.6 collective-permute-start.43
  207.7 4.3 collective-permute-start.44
  212.2 10.5 %collective-permute-start.47 = (f32[8,16,1]{2,1,0:T(8,128)S(1)}, f32[8,16,1]{2,1,0:T(8,128)S(1)}, u32[]{:S(2)}, u32[]{:S(2)}) collective-permute-start(f32[8,16,1]{2,1,0:T(8,128)S(1)} %slice.739), channel_id=1, source_target_pairs={{0,2},{2,4},{4,6},{6,8},{8,10},{10,12},{12,14},{14,16},{16,18},{18... | collective-permute-start | bytes 1544 | tf_op jit(solution)/shard_map/ppermute | solution.py:38
  218.8 10.3 %collective-permute-start.46 = (f32[8,1,128]{2,1,0:T(1,128)S(1)}, f32[8,1,128]{2,1,0:T(1,128)S(1)}, u32[]{:S(2)}, u32[]{:S(2)}) collective-permute-start(f32[8,1,128]{2,1,0:T(1,128)S(1)} %slice.737), channel_id=1, source_target_pairs={{0,32},{32,64},{64,96},{96,128},{128,160},{160,192},{192,224},{224... | collective-permute-start | bytes 12296 | tf_op jit(solution)/shard_map/ppermute | solution.py:38
  231.6 236.9 %all-reduce.3.cloned.1.call-start = ((), (), s32[]{:S(2)}) async-start(), calls=%async_computation.2 | async-start | bytes 1048576 | tf_op jit(solution)/shard_map/psum | solution.py:168
  261.3 379.4 %all-reduce.5.cloned.1.call-start = ((), (), s32[]{:S(2)}) async-start(), calls=%async_computation.3 | async-start | bytes 1048576 | tf_op jit(solution)/shard_map/psum | solution.py:168
  (10 other events, 84.6 us)
Sparse Core Ops, SparseCore 0:
  231.8 16.1 reduce-scatter.1
  261.5 207.0 all-reduce.2
  471.4 169.2 all-reduce.4
